TPU v7x, 512 devices: a whole 4x8x8 slice. The times are simulated.
512 devices in a mesh: dp: 16 (over x, z_hi), tm: 32 (over z_lo, y, core).
Axes of the slice: x: 4, y: 8, z: 8 (z_hi: 4, z_lo: 2; z = z_hi * 2 + z_lo), core: 2. Of those that a mesh axis runs over, the one named last changes fastest.
Arguments:
- activations: bfloat16 [16, 64, 64, 16, 128], P('dp', 'tm')
- conv_weight: bfloat16 [3, 3, 3, 128, 128], replicated, may hold values from -0.109375 to 0.109375
- norm_gain: float32 [128], replicated, may hold values from 0.5 to 1.5
- norm_bias: float32 [128], replicated, may hold values from -0.5 to 0.5
- down_weight: bfloat16 [3, 3, 128, 128], replicated, may hold values from -0.1875 to 0.1875
- cotangent: bfloat16 [16, 64, 32, 8, 128], P('dp', None, 'tm'), may hold values from -0.21875 to 0.21875
Outputs:
- encoded: bfloat16 [16, 64, 32, 8, 128], P('dp', None, 'tm')
- grad_down: float32 [3, 3, 128, 128], P(None, None, None, 'tm')
All inputs are finite; a program needn't handle non-finite values.
Results may differ from a plain program's by a relative error of at most 0.005.
Values may be sent and summed in bfloat16 or wider, within the bound.
A program may use at most 64 MiB of HBM per device.

v0:
```python
import jax
import jax.numpy as jnp
from jax import lax
from jax.sharding import PartitionSpec as P

G = 32


def passed_along(shard, axis, by):
    count = lax.axis_size(axis)
    pairs = [(i, i + by) for i in range(count) if 0 <= i + by < count]
    return lax.ppermute(shard, axis, pairs)


def down_patches(extended, rows_out, cols_out):
    tap_list = []
    for row_tap in range(3):
        for col_tap in range(3):
            tap_list.append(
                extended[
                    :,
                    :,
                    row_tap : row_tap + 2 * rows_out - 1 : 2,
                    col_tap : col_tap + 2 * cols_out - 1 : 2,
                    :,
                ]
            )
    return jnp.concatenate(tap_list, axis=-1)


def per_device(activations, conv_weight, norm_gain, norm_bias, down_weight, cotangent):
    clip_count, frames_dev, height, width_cells, channels = activations.shape
    out_channels = conv_weight.shape[-1]
    groups = G
    earlier = passed_along(activations, "tm", 1)
    framed = jnp.concatenate([earlier, activations], axis=1)
    framed = jnp.pad(framed, ((0, 0), (0, 0), (1, 1), (1, 1), (0, 0)))
    conv_out = jnp.zeros(
        (clip_count * frames_dev * height * width_cells, out_channels), jnp.float32
    )
    for row_tap in range(3):
        for col_tap in range(3):
            window_slab = framed[
                :, :, row_tap : row_tap + height, col_tap : col_tap + width_cells, :
            ]
            stacked = jnp.concatenate(
                [window_slab[:, time_tap : time_tap + frames_dev] for time_tap in range(3)], axis=-1
            )
            tap_weight = conv_weight[:, row_tap, col_tap].reshape(3 * channels, out_channels)
            conv_out = conv_out + jnp.dot(
                stacked.reshape(-1, 3 * channels), tap_weight, preferred_element_type=jnp.float32
            )
    grouped = conv_out.reshape(
        clip_count, frames_dev, height, width_cells, groups, channels // groups
    )
    group_sums = jnp.sum(grouped, axis=(1, 2, 3, 5))
    group_squares = jnp.sum(grouped * grouped, axis=(1, 2, 3, 5))
    group_sums, group_squares = lax.psum((group_sums, group_squares), "tm")
    members = float(frames_dev * lax.axis_size("tm") * height * width_cells * (channels // groups))
    group_mean = group_sums / members
    variance = group_squares / members - group_mean * group_mean
    inverse = lax.rsqrt(variance + 1e-06)
    normed = (
        (grouped - group_mean[:, None, None, None, :, None]) * inverse[:, None, None, None, :, None]
    ).reshape(clip_count, frames_dev, height, width_cells, channels) * norm_gain + norm_bias
    hidden = jax.nn.silu(normed).astype(jnp.bfloat16)
    down_flat = down_weight.reshape(9 * channels, -1)
    row_local = lax.all_to_all(hidden, "tm", split_axis=2, concat_axis=1, tiled=True)
    lower_row = passed_along(row_local[:, :, :1], "tm", -1)
    extended = jnp.concatenate([row_local, lower_row], axis=2)
    extended = jnp.pad(extended, ((0, 0), (0, 0), (0, 0), (0, 1), (0, 0)))
    patches = down_patches(extended, row_local.shape[2] // 2, width_cells // 2)
    encoded = (
        jnp.dot(patches.reshape(-1, 9 * channels), down_flat, preferred_element_type=jnp.float32)
        .reshape(cotangent.shape)
        .astype(jnp.bfloat16)
    )
    partial_value = lax.dot_general(
        patches.reshape(-1, 9 * channels),
        cotangent.reshape(-1, cotangent.shape[-1]),
        (((0,), (0,)), ((), ())),
        preferred_element_type=jnp.float32,
    )
    partial_value = partial_value.reshape(3, 3, channels, -1)
    shares = lax.psum_scatter(partial_value, "tm", scatter_dimension=3, tiled=True)
    grad_down = lax.psum(shares, "dp")
    return (encoded, grad_down)


def solution(mesh):
    placed = (P("dp", "tm", None, None, None), P(), P(), P(), P(), P("dp", None, "tm", None, None))
    return jax.shard_map(
        per_device,
        mesh=mesh,
        in_specs=placed,
        out_specs=(P("dp", None, "tm", None, None), P(None, None, None, "tm")),
        check_vma=False,
    )
```

profile of v0, /device:TPU:64, one launch (start us, length us, event | category | flops | bytes accessed | tf_op | source)
XLA Modules:
  0.0 432.4 jit_solution(16287270471883125071)
XLA Ops:
  7.2 2.1 collective-permute-start
  9.3 1.3 fusion.17
  10.6 9.6 %collective-permute-done = bf16[1,2,64,16,128]{4,3,2,1,0:T(8,128)(2,1)S(1)} collective-permute-done((bf16[1,2,64,16,128]{4,3,2,1,0:T(8,128)(2,1)}, bf16[1,2,64,16,128]{4,3,2,1,0:T(8,128)(2,1)S(1)}, u32[]{:S(2)}, u32[]{:S(2)}) %collective-permute-start) | collective-permute-done | bytes 524320 | tf_op jit(solution)/shard_map/ppermute | solution.py:12
  20.3 3.1 pad_slice_fusion.2
  23.4 0.6 pad_slice_fusion.1
  24.0 0.4 pad_maximum_fusion
  24.5 0.6 fusion.18
  25.1 0.6 convolution_add_fusion.7
  26.1 0.6 convolution_add_fusion.6
  26.7 0.6 convolution_add_fusion.5
  27.5 0.6 convolution_add_fusion.4
  28.5 0.6 convolution_add_fusion.3
  29.1 0.6 convolution_add_fusion.2
  29.7 0.4 pad_maximum_fusion.7
  30.1 0.6 convolution_add_fusion.1
  30.7 0.7 fusion.16
  31.9 53.0 %all-reduce.3 = (f32[1,32]{1,0:T(1,128)S(1)}, f32[1,32]{1,0:T(1,128)S(1)}) all-reduce(f32[1,32]{1,0:T(1,128)S(1)} %bitcast.101, f32[1,32]{1,0:T(1,128)S(1)} %bitcast.100), channel_id=1, replica_groups=mesh['dp'=16,'tm'=32] {'tm'}, use_global_device_ids=true, to_apply=%region_5.6 | all-reduce | flops 64 | bytes 512 | tf_op jit(solution)/shard_map/psum | solution.py:58
  85.6 20.5 %all_to_all.18 = bf16[1,2,64,16,128]{4,3,1,0,2:T(8,128)(2,1)S(1)} all-to-all(bf16[1,2,64,16,128]{4,3,1,0,2:T(8,128)(2,1)S(1)} %multiply_convert_fusion), channel_id=1, replica_groups=mesh['dp'=16,'tm'=32] {'tm'}, dimensions={2} | all-to-all | bytes 1048576 | tf_op jit(solution)/shard_map/all_to_all | solution.py:68
  106.1 2.1 collective-permute-start.1
  108.2 3.7 collective-permute-done.1
  112.9 0.7 slice.213
  113.6 0.4 slice.214
  114.1 0.4 slice.215
  114.5 0.7 slice.216
  116.0 0.7 slice.219
  117.1 0.6 copy.18
  117.9 1.3 fusion.14
  119.2 1.3 dynamic-slice
  121.1 1.1 fusion.8
  122.3 220.0 %all-reduce.6.cloned.1.call-done = f32[3,3,128,128]{2,3,1,0:T(8,128)} async-done(((f32[3,3,128,128]{2,3,1,0:T(8,128)}), f32[3,3,128,128]{2,3,1,0:T(8,128)}) %all-reduce.6.cloned.1.call-update) | async-done | bytes 589840
  342.3 0.8 constant_dynamic-slice_fusion
  343.0 82.5 %psum.23 = f32[3,3,128,4]{2,3,1,0:T(4,128)} all-reduce(f32[3,3,128,4]{2,3,1,0:T(4,128)S(1)} %constant_dynamic-slice_fusion), channel_id=1, replica_groups=mesh['dp'=16,'tm'=32] {'dp'}, use_global_device_ids=true, to_apply=%region_7.8 | all-reduce | flops 4608 | bytes 36864 | tf_op jit(solution)/shard_map/psum | solution.py:86
  (43 shorter events, 4.7 us)
Async XLA Ops:
  7.2 114.0 %copy-start = (bf16[3,3,128,128]{3,2,1,0:T(8,128)(2,1)S(1)}, bf16[3,3,128,128]{3,2,1,0:T(8,128)(2,1)}, u32[]{:S(2)}) copy-start(bf16[3,3,128,128]{3,2,1,0:T(8,128)(2,1)} %param.10) | copy-start | bytes 884740
  7.2 13.0 %copy-start.1 = (bf16[1,2,64,16,128]{4,3,2,1,0:T(8,128)(2,1)S(1)}, bf16[1,2,64,16,128]{4,3,2,1,0:T(8,128)(2,1)}, u32[]{:S(2)}) copy-start(bf16[1,2,64,16,128]{4,3,2,1,0:T(8,128)(2,1)} %param.6) | copy-start | bytes 1572868
  7.2 335.1 %all-reduce.6.cloned.1.call-start = ((), (), s32[]{:S(2)}) async-start(), calls=%async_computation.1 | async-start | bytes 1179648
  7.2 13.0 %collective-permute-start = (bf16[1,2,64,16,128]{4,3,2,1,0:T(8,128)(2,1)}, bf16[1,2,64,16,128]{4,3,2,1,0:T(8,128)(2,1)S(1)}, u32[]{:S(2)}, u32[]{:S(2)}) collective-permute-start(bf16[1,2,64,16,128]{4,3,2,1,0:T(8,128)(2,1)} %param.6), channel_id=1, source_target_pairs={{0,1},{1,2},{2,3},{3,4},{4,5},{5,6},{6,7},{7,8},{8,9},{9,10},{10,1... | collective-permute-start | bytes 1572872 | tf_op jit(solution)/shard_map/ppermute | solution.py:12
  30.7 54.5 %copy-start.3 = (f32[128]{0:T(128)S(1)}, f32[128]{0:T(128)}, u32[]{:S(2)}) copy-start(f32[128]{0:T(128)} %param.9) | copy-start | bytes 1540
  30.7 54.5 %copy-start.4 = (f32[128]{0:T(128)S(1)}, f32[128]{0:T(128)}, u32[]{:S(2)}) copy-start(f32[128]{0:T(128)} %param.8) | copy-start | bytes 1540
  106.1 5.8 %collective-permute-start.1 = (bf16[1,64,1,16,128]{4,3,1,2,0:T(8,128)(2,1)S(1)}, bf16[1,64,1,16,128]{4,3,1,2,0:T(8,128)(2,1)S(1)}, u32[]{:S(2)}, u32[]{:S(2)}) collective-permute-start(bf16[1,64,1,16,128]{4,3,1,2,0:T(8,128)(2,1)S(1)} %slice.221), channel_id=1, source_target_pairs={{1,0},{2,1},{3,2},{4,3},{5,4},{6,5},{7,6},{8,7},{9,8},{10,9},{11,1... | collective-permute-start | bytes 786440 | tf_op jit(solution)/shard_map/ppermute | solution.py:12
  117.0 0.9 copy-start.2
Sparse Core Ops, SparseCore 0:
  119.3 222.8 all-reduce.5
where the time goes:
time: 433 us; the launch traced here: 432 us
  waiting for transfers between devices  233 us (54%)
  blocking collectives  156 us (36%)
  between operations  15.1 us (3%)
  local copies, waits for them, and re-layouts  13.4 us (3%)
  matrix products  7.8 us (2%)
    unnamed x2, waiting for transfers between devices  220 us
    psum x1, blocking collectives, per_device(): grad_down = lax.psum(shares, 'dp')  82.5 us
    psum x1, blocking collectives, per_device(): group_sums, group_squares = lax.psum((group_sums, group_squares), 'tm')  53 us
    all_to_all x1, blocking collectives, per_device(): lax.all_to_all(hidden, 'tm', split_axis=2, concat_axis=1, tiled=True)  20.5 us
    ppermute x2, waiting for transfers between devices, passed_along(): return lax.ppermute(shard, axis, pairs)  13.3 us
  transfers between devices with their start and end apart: 3, of which 3 were waited for; matrix products, arithmetic and copies ran while one was open for 1% of the time, Pallas kernels for 0%

commit v1 on v0

--- a/solution.py
+++ b/solution.py
@@ -83,7 +83,8 @@
     )
     partial_value = partial_value.reshape(3, 3, channels, -1)
     shares = lax.psum_scatter(partial_value, "tm", scatter_dimension=3, tiled=True)
-    grad_down = lax.psum(shares, "dp")
+    parts = lax.all_gather(shares, "dp")
+    grad_down = jnp.sum(parts, axis=0)
     return (encoded, grad_down)
 
 

time: 433 us -> 396 us (0.915)
  blocking collectives: 156 us -> 119 us
    psum x1 -> x0, blocking collectives: 82.5 us -> none  [per_device(): grad_down = lax.psum(shares, 'dp')]
    all_gather x0 -> x1, blocking collectives: none -> 45.4 us  [per_device(): parts = lax.all_gather(shares, 'dp')]
where the time goes in v1:
time: 396 us
  waiting for transfers between devices  233 us (59%)
  blocking collectives  119 us (30%)
  between operations  15.1 us (4%)
  local copies, waits for them, and re-layouts  13.4 us (3%)
  matrix products  7.8 us (2%)
  starting transfers between devices  4.19 us (1%)
    unnamed x2, waiting for transfers between devices  220 us
    psum x1, blocking collectives, per_device(): group_sums, group_squares = lax.psum((group_sums, group_squares), 'tm')  53 us
    all_gather x1, blocking collectives, per_device(): parts = lax.all_gather(shares, 'dp')  45.4 us
    all_to_all x1, blocking collectives, per_device(): lax.all_to_all(hidden, 'tm', split_axis=2, concat_axis=1, tiled=True)  20.5 us
    ppermute x2, waiting for transfers between devices, passed_along(): return lax.ppermute(shard, axis, pairs)  13.3 us
  transfers between devices with their start and end apart: 3, of which 3 were waited for; matrix products, arithmetic and copies ran while one was open for 1% of the time, Pallas kernels for 0%

profile of v1, /device:TPU:64, one launch (start us, length us, event | category | flops | bytes accessed | tf_op | source)
XLA Modules:
  0.0 396.0 jit_solution(2410299195833913455)
XLA Ops:
  7.2 2.1 collective-permute-start
  9.3 1.3 fusion.17
  10.6 9.6 %collective-permute-done = bf16[1,2,64,16,128]{4,3,2,1,0:T(8,128)(2,1)S(1)} collective-permute-done((bf16[1,2,64,16,128]{4,3,2,1,0:T(8,128)(2,1)}, bf16[1,2,64,16,128]{4,3,2,1,0:T(8,128)(2,1)S(1)}, u32[]{:S(2)}, u32[]{:S(2)}) %collective-permute-start) | collective-permute-done | bytes 524320 | tf_op jit(solution)/shard_map/ppermute | solution.py:12
  20.3 3.1 pad_slice_fusion.2
  23.4 0.6 pad_slice_fusion.1
  24.0 0.4 pad_maximum_fusion
  24.5 0.6 fusion.18
  25.1 0.6 convolution_add_fusion.7
  26.1 0.6 convolution_add_fusion.6
  26.7 0.6 convolution_add_fusion.5
  27.5 0.6 convolution_add_fusion.4
  28.5 0.6 convolution_add_fusion.3
  29.1 0.6 convolution_add_fusion.2
  29.7 0.4 pad_maximum_fusion.7
  30.1 0.6 convolution_add_fusion.1
  30.7 0.7 fusion.16
  31.9 53.0 %all-reduce.3 = (f32[1,32]{1,0:T(1,128)S(1)}, f32[1,32]{1,0:T(1,128)S(1)}) all-reduce(f32[1,32]{1,0:T(1,128)S(1)} %bitcast.103, f32[1,32]{1,0:T(1,128)S(1)} %bitcast.102), channel_id=1, replica_groups=mesh['dp'=16,'tm'=32] {'tm'}, use_global_device_ids=true, to_apply=%region_5.6 | all-reduce | flops 64 | bytes 512 | tf_op jit(solution)/shard_map/psum | solution.py:58
  85.6 20.5 %all_to_all.18 = bf16[1,2,64,16,128]{4,3,1,0,2:T(8,128)(2,1)S(1)} all-to-all(bf16[1,2,64,16,128]{4,3,1,0,2:T(8,128)(2,1)S(1)} %multiply_convert_fusion), channel_id=1, replica_groups=mesh['dp'=16,'tm'=32] {'tm'}, dimensions={2} | all-to-all | bytes 1048576 | tf_op jit(solution)/shard_map/all_to_all | solution.py:68
  106.1 2.1 collective-permute-start.1
  108.2 3.7 collective-permute-done.1
  112.9 0.7 slice.213
  113.6 0.4 slice.214
  114.5 0.7 slice.216
  116.0 0.7 slice.219
  117.1 0.6 copy.18
  117.9 1.3 fusion.14
  119.2 1.3 dynamic-slice
  121.1 1.1 fusion.8
  122.3 220.0 %all-reduce.6.cloned.1.call-done = f32[3,3,128,128]{2,3,1,0:T(8,128)} async-done(((f32[3,3,128,128]{2,3,1,0:T(8,128)}), f32[3,3,128,128]{2,3,1,0:T(8,128)}) %all-reduce.6.cloned.1.call-update) | async-done | bytes 589840
  342.3 0.8 constant_dynamic-slice_fusion
  343.0 45.4 %all-gather = f32[48,3,128,4]{2,3,1,0:T(4,128)S(1)} all-gather(f32[3,3,128,4]{2,3,1,0:T(4,128)S(1)} %constant_dynamic-slice_fusion), channel_id=2, replica_groups=mesh['dp'=16,'tm'=32] {'dp'}, dimensions={0}, use_global_device_ids=true | all-gather | bytes 313344 | tf_op jit(solution)/shard_map/all_gather | solution.py:86
  388.5 0.7 reduce_sum.53
  (44 shorter events, 5.1 us)
Async XLA Ops:
  7.2 114.0 %copy-start = (bf16[3,3,128,128]{3,2,1,0:T(8,128)(2,1)S(1)}, bf16[3,3,128,128]{3,2,1,0:T(8,128)(2,1)}, u32[]{:S(2)}) copy-start(bf16[3,3,128,128]{3,2,1,0:T(8,128)(2,1)} %param.10) | copy-start | bytes 884740
  7.2 13.0 %copy-start.1 = (bf16[1,2,64,16,128]{4,3,2,1,0:T(8,128)(2,1)S(1)}, bf16[1,2,64,16,128]{4,3,2,1,0:T(8,128)(2,1)}, u32[]{:S(2)}) copy-start(bf16[1,2,64,16,128]{4,3,2,1,0:T(8,128)(2,1)} %param.6) | copy-start | bytes 1572868
  7.2 335.1 %all-reduce.6.cloned.1.call-start = ((), (), s32[]{:S(2)}) async-start(), calls=%async_computation.1 | async-start | bytes 1179648
  7.2 13.0 %collective-permute-start = (bf16[1,2,64,16,128]{4,3,2,1,0:T(8,128)(2,1)}, bf16[1,2,64,16,128]{4,3,2,1,0:T(8,128)(2,1)S(1)}, u32[]{:S(2)}, u32[]{:S(2)}) collective-permute-start(bf16[1,2,64,16,128]{4,3,2,1,0:T(8,128)(2,1)} %param.6), channel_id=1, source_target_pairs={{0,1},{1,2},{2,3},{3,4},{4,5},{5,6},{6,7},{7,8},{8,9},{9,10},{10,1... | collective-permute-start | bytes 1572872 | tf_op jit(solution)/shard_map/ppermute | solution.py:12
  30.7 54.5 %copy-start.3 = (f32[128]{0:T(128)S(1)}, f32[128]{0:T(128)}, u32[]{:S(2)}) copy-start(f32[128]{0:T(128)} %param.9) | copy-start | bytes 1540
  30.7 54.5 %copy-start.4 = (f32[128]{0:T(128)S(1)}, f32[128]{0:T(128)}, u32[]{:S(2)}) copy-start(f32[128]{0:T(128)} %param.8) | copy-start | bytes 1540
  106.1 5.8 %collective-permute-start.1 = (bf16[1,64,1,16,128]{4,3,1,2,0:T(8,128)(2,1)S(1)}, bf16[1,64,1,16,128]{4,3,1,2,0:T(8,128)(2,1)S(1)}, u32[]{:S(2)}, u32[]{:S(2)}) collective-permute-start(bf16[1,64,1,16,128]{4,3,1,2,0:T(8,128)(2,1)S(1)} %slice.221), channel_id=1, source_target_pairs={{1,0},{2,1},{3,2},{4,3},{5,4},{6,5},{7,6},{8,7},{9,8},{10,9},{11,1... | collective-permute-start | bytes 786440 | tf_op jit(solution)/shard_map/ppermute | solution.py:12
  117.0 0.9 copy-start.2
Sparse Core Ops, SparseCore 0:
  119.3 222.8 all-reduce.5
